TPU v7x, 32 devices: a whole 2x2x4 slice. The times are simulated.
32 devices in a mesh: section: 4 (over z), row: 2 (over x), col: 4 (over y, core).
Axes of the slice: x: 2, y: 2, z: 4, core: 2. Of those that a mesh axis runs over, the one named last changes fastest.
Arguments:
- input_fwd: bfloat16 [4, 256, 2560], P('section', 'col', 'row'), may hold values from -6 to 6
- input_bwd: bfloat16 [4, 256, 2560], P('section', 'col', 'row'), may hold values from -6 to 6
- cotangent: bfloat16 [4, 256, 2560], P('section', 'col', 'row'), may hold values from -0.375 to 0.375
- shared_up: bfloat16 [2560, 16384], P('row', ('col', 'section')), may hold values from -0.125 to 0.125
- shared_down: bfloat16 [16384, 2560], P(('col', 'section'), 'row'), may hold values from -0.046875 to 0.046875
- up_left: bfloat16 [4, 2560, 256], P('section', 'row'), may hold values from -0.125 to 0.125
- up_right: bfloat16 [4, 256, 16384], P('section', None, 'col'), may hold values from -0.1875 to 0.1875
- down_left: bfloat16 [4, 16384, 256], P('section', 'col'), may hold values from -0.046875 to 0.046875
- down_right: bfloat16 [4, 256, 2560], P('section', None, 'row'), may hold values from -0.1875 to 0.1875
Outputs:
- handoff_fwd: bfloat16 [4, 256, 2560], P('section', 'col', 'row')
- handoff_bwd: bfloat16 [4, 256, 2560], P('section', 'col', 'row')
- grad_shared_up: bfloat16 [2560, 16384], P('row', ('col', 'section'))
- grad_shared_down: bfloat16 [16384, 2560], P(('col', 'section'), 'row')
- grad_up_left: float32 [4, 2560, 256], P('section', 'row')
- grad_up_right: float32 [4, 256, 16384], P('section', None, 'col')
- grad_down_left: float32 [4, 16384, 256], P('section', 'col')
- grad_down_right: float32 [4, 256, 2560], P('section', None, 'row')
All inputs are finite; a program needn't handle non-finite values.
Results may differ from a plain program's by a relative error of at most 0.022.
Values may be sent and summed in bfloat16 or wider, within the bound.
A program may use at most 128 MiB of HBM per device.

v0:
```python
import jax
import jax.numpy as jnp
from jax import lax
from jax.sharding import PartitionSpec as P


def from_behind(block, axis, distance):
    devices = range(lax.axis_size(axis))
    route = [((i - distance) % len(devices), i) for i in devices]
    return lax.ppermute(block, axis, route)


def silu_slope(preact):
    sigma = jax.nn.sigmoid(preact)
    return sigma * (1.0 + preact * (1.0 - sigma))


def local(
    input_fwd,
    input_bwd,
    cotangent,
    shared_up,
    shared_down,
    up_left,
    up_right,
    down_left,
    down_right,
):
    own_rows = input_fwd.shape[1]
    row_start = lax.axis_index("col") * own_rows
    full_up, full_down = (
        lax.all_gather(shared_up, "section", axis=1, tiled=True),
        lax.all_gather(shared_down, "section", axis=0, tiled=True),
    )
    in_left = up_left[0]
    in_right = up_right[0]
    out_left = down_left[0]
    out_right = down_right[0]
    stacked = jnp.stack([input_fwd[0], input_bwd[0]])
    normed_all = lax.all_gather(stacked, "col", axis=1, tiled=True)
    up_part = jnp.einsum("tmd,df->tmf", normed_all, full_up, preferred_element_type=jnp.float32)
    din_part = jnp.einsum("tmd,dr->tmr", normed_all, in_left, preferred_element_type=jnp.float32)
    preact, din_sum = (
        lax.psum(up_part.astype(jnp.bfloat16), "row").astype(jnp.float32),
        lax.psum(din_part.astype(jnp.bfloat16), "row").astype(jnp.float32),
    )
    delta_in = din_sum.astype(jnp.bfloat16)
    preact = preact + jnp.einsum(
        "tmr,rf->tmf", delta_in, in_right, preferred_element_type=jnp.float32
    )
    hidden = jax.nn.silu(preact).astype(jnp.bfloat16)
    dout_part = jnp.einsum("tmf,fr->tmr", hidden, out_left, preferred_element_type=jnp.float32)
    down_part = jnp.dot(hidden[0], full_down, preferred_element_type=jnp.float32)
    down_own = lax.psum_scatter(
        down_part.astype(jnp.bfloat16), "col", scatter_dimension=0, tiled=True
    ).astype(jnp.float32)
    delta_out = lax.psum(dout_part.astype(jnp.bfloat16), "col")
    dout_own = lax.dynamic_slice_in_dim(delta_out[0], row_start, own_rows, 0)
    out_fwd = (
        input_fwd[0].astype(jnp.float32)
        + down_own
        + jnp.dot(dout_own, out_right, preferred_element_type=jnp.float32)
    )
    handoff_fwd = from_behind(out_fwd.astype(jnp.bfloat16)[None], "section", 1)
    cot_all = lax.all_gather(cotangent[0], "col", axis=0, tiled=True)
    hidden_bwd = hidden[1]
    normed_bwd = normed_all[1]
    grad_down_right = jnp.einsum(
        "mr,md->rd", delta_out[1], cot_all, preferred_element_type=jnp.float32
    )
    grad_down = jnp.einsum("mf,md->fd", hidden_bwd, cot_all, preferred_element_type=jnp.float32)
    gdout_part = jnp.einsum("md,rd->mr", cot_all, out_right, preferred_element_type=jnp.float32)
    ghid_part = jnp.einsum("md,fd->mf", cot_all, full_down, preferred_element_type=jnp.float32)
    grad_hidden, gdout_sum = (
        lax.psum(ghid_part.astype(jnp.bfloat16), "row").astype(jnp.float32),
        lax.psum(gdout_part.astype(jnp.bfloat16), "row").astype(jnp.float32),
    )
    grad_dout = gdout_sum.astype(jnp.bfloat16)
    grad_hidden = grad_hidden + jnp.einsum(
        "mr,fr->mf", grad_dout, out_left, preferred_element_type=jnp.float32
    )
    grad_preact = (grad_hidden * silu_slope(preact[1])).astype(jnp.bfloat16)
    grad_down_left = jnp.einsum(
        "mf,mr->fr", hidden_bwd, grad_dout, preferred_element_type=jnp.float32
    )
    grad_up = jnp.einsum("md,mf->df", normed_bwd, grad_preact, preferred_element_type=jnp.float32)
    grad_up_right = jnp.einsum(
        "mr,mf->rf", delta_in[1], grad_preact, preferred_element_type=jnp.float32
    )
    gdin_part = jnp.einsum("mf,rf->mr", grad_preact, in_right, preferred_element_type=jnp.float32)
    gnorm_part = jnp.einsum("mf,df->md", grad_preact, full_up, preferred_element_type=jnp.float32)
    grad_normed = lax.psum_scatter(
        gnorm_part.astype(jnp.bfloat16), "col", scatter_dimension=0, tiled=True
    ).astype(jnp.float32)
    grad_din = lax.psum(gdin_part.astype(jnp.bfloat16), "col")
    grad_up_left = jnp.einsum("md,mr->dr", normed_bwd, grad_din, preferred_element_type=jnp.float32)
    gdin_own = lax.dynamic_slice_in_dim(grad_din, row_start, own_rows, 0)
    grad_normed = grad_normed + jnp.einsum(
        "mr,dr->md", gdin_own, in_left, preferred_element_type=jnp.float32
    )
    grad_input = cotangent[0].astype(jnp.float32) + grad_normed
    handoff_bwd = from_behind(grad_input.astype(jnp.bfloat16)[None], "section", -1)
    sum_up, sum_down = (
        lax.psum_scatter(
            grad_up.astype(jnp.bfloat16), "section", scatter_dimension=1, tiled=True
        ).astype(jnp.float32),
        lax.psum_scatter(
            grad_down.astype(jnp.bfloat16), "section", scatter_dimension=0, tiled=True
        ).astype(jnp.float32),
    )
    return (
        handoff_fwd,
        handoff_bwd,
        sum_up.astype(jnp.bfloat16),
        sum_down.astype(jnp.bfloat16),
        grad_up_left[None],
        grad_up_right[None],
        grad_down_left[None],
        grad_down_right[None],
    )


def solution(mesh):
    in_specs = (
        P("section", "col", "row"),
        P("section", "col", "row"),
        P("section", "col", "row"),
        P("row", ("col", "section")),
        P(("col", "section"), "row"),
        P("section", "row", None),
        P("section", None, "col"),
        P("section", "col", None),
        P("section", None, "row"),
    )
    out_specs = (
        P("section", "col", "row"),
        P("section", "col", "row"),
        P("row", ("col", "section")),
        P(("col", "section"), "row"),
        P("section", "row", None),
        P("section", None, "col"),
        P("section", "col", None),
        P("section", None, "row"),
    )
    return jax.shard_map(local, mesh=mesh, in_specs=in_specs, out_specs=out_specs, check_vma=False)
```

profile of v0, /device:TPU:0, one launch (start us, length us, event | category | flops | bytes accessed | tf_op | source)
XLA Modules:
  0.0 1039.4 jit_solution(6350049642316456893)
XLA Ops:
  7.2 1.9 pad_maximum_fusion
  10.7 9.6 all-gather
  21.4 9.7 all-gather.5.cloned.1.call-done
  31.1 2.7 convolution_convert_fusion.5
  33.8 182.8 %all-gather.7.cloned.1.call-done = bf16[1280,4096]{1,0:T(8,128)(2,1)} async-done(((bf16[1280,1024]{1,0:T(8,128)(2,1)}), bf16[1280,4096]{1,0:T(8,128)(2,1)}) %all-gather.7.cloned.1.call-update) | async-done | bytes 10485776 | tf_op jit(solution)/shard_map/all_gather | solution.py:32
  216.6 10.0 fusion.2
  226.5 173.7 %all-gather.9.cloned.1.call-done = bf16[4096,1280]{1,0:T(8,128)(2,1)} async-done(((bf16[1024,1280]{1,0:T(8,128)(2,1)}), bf16[4096,1280]{1,0:T(8,128)(2,1)}) %all-gather.9.cloned.1.call-update) | async-done | bytes 10485776 | tf_op jit(solution)/shard_map/all_gather | solution.py:33
  400.3 12.0 %convolution_convert_fusion.2 = bf16[256,4096]{1,0:T(8,128)(2,1)} fusion(bf16[4096,1280]{1,0:T(8,128)(2,1)} %all-gather.9.cloned.1.call-done, bf16[1,256,1280]{2,1,0:T(8,128)(2,1)S(1)} %all-gather), kind=kOutput, calls=%fused_computation.12 | convolution fusion | flops 2685403136 | bytes 13238272 | tf_op jit(solution)/shard_map/md,fd->mf/dot_general | solution.py:73
  412.3 160.1 %all-reduce.7.cloned.1.call-done = (bf16[2,256,4096]{2,1,0:T(8,128)(2,1)}, bf16[2,256,256]{2,1,0:T(8,128)(2,1)}, bf16[256,256]{1,0:T(8,128)(2,1)}, bf16[256,4096]{1,0:T(8,128)(2,1)}) async-done(((bf16[2,256,4096]{2,1,0:T(8,128)(2,1)}, bf16[2,256,256]{2,1,0:T(8,128)(2,1)}, bf16[256,256]{1,0:T(8,128)(2,1)}, bf16[256,4096]{1,0:T(8,128)(2,1)}), (bf16[2,256,4096]{2,1,0:T(8,128)(2,1)}, ...) | async-done | bytes 6684688 | tf_op jit(solution)/shard_map/psum | solution.py:44
  572.4 4.6 multiply_convert_fusion
  577.0 2.0 fusion.18
  579.0 1.3 copy-done.10
  580.3 2.1 fusion.6
  582.4 1.3 copy-done.4
  583.7 1.4 fusion.21
  585.2 8.5 convolution_convert_fusion.4
  593.9 7.8 convolution_convert_fusion.3
  601.8 6.7 convolution_convert_fusion
  608.5 8.4 convolution_convert_fusion.1
  617.0 3.8 convolution_bitcast_fusion.1
  620.8 2.8 convolution_bitcast_fusion
  623.6 1.6 slice.29
  625.2 2.3 convolution_bitcast_fusion.2
  627.5 16.0 %reduce-scatter.5.cloned.1.call-done = bf16[64,1280]{1,0:T(8,128)(2,1)} async-done(((bf16[256,1280]{1,0:T(8,128)(2,1)}), bf16[64,1280]{1,0:T(8,128)(2,1)}) %reduce-scatter.5.cloned.1.call-update) | async-done | bytes 163856 | tf_op jit(solution)/shard_map/reduce_scatter | solution.py:54
  643.5 1.3 fusion.10
  644.8 1.5 collective-permute-start
  646.3 22.1 %reduce-scatter.7.cloned.1.call-done = bf16[64,1280]{1,0:T(8,128)(2,1)} async-done(((bf16[256,1280]{1,0:T(8,128)(2,1)}), bf16[64,1280]{1,0:T(8,128)(2,1)}) %reduce-scatter.7.cloned.1.call-update) | async-done | bytes 163856 | tf_op jit(solution)/shard_map/reduce_scatter | solution.py:92
  668.5 1.5 fusion.11
  670.0 3.4 collective-permute-start.1
  673.4 2.5 convolution_bitcast_fusion.3
  676.7 172.8 %reduce-scatter.9.cloned.1.call-done = bf16[1280,1024]{1,0:T(8,128)(2,1)} async-done(((bf16[1280,4096]{1,0:T(8,128)(2,1)}), bf16[1280,1024]{1,0:T(8,128)(2,1)}) %reduce-scatter.9.cloned.1.call-update) | async-done | bytes 2621456 | tf_op jit(solution)/shard_map/reduce_scatter | solution.py:104
  849.5 182.0 %reduce-scatter.11.cloned.1.call-done = bf16[1024,1280]{1,0:T(8,128)(2,1)} async-done(((bf16[4096,1280]{1,0:T(8,128)(2,1)}), bf16[1024,1280]{1,0:T(8,128)(2,1)}) %reduce-scatter.11.cloned.1.call-update) | async-done | bytes 2621456 | tf_op jit(solution)/shard_map/reduce_scatter | solution.py:107
  (44 shorter events, 5.2 us)
Async XLA Ops:
  7.2 565.2 %copy-start = (bf16[1,256,4096]{2,1,0:T(8,128)(2,1)S(1)}, bf16[1,256,4096]{2,1,0:T(8,128)(2,1)}, u32[]{:S(2)}) copy-start(bf16[1,256,4096]{2,1,0:T(8,128)(2,1)} %param.15) | copy-start | bytes 6291460
  7.2 13.1 %copy-start.6 = (bf16[1,256,1280]{2,1,0:T(8,128)(2,1)S(1)}, bf16[1,256,1280]{2,1,0:T(8,128)(2,1)}, u32[]{:S(2)}) copy-start(bf16[1,256,1280]{2,1,0:T(8,128)(2,1)} %param.17) | copy-start | bytes 1966084
  7.2 23.9 %all-gather.5.cloned.1.call-start = ((), (), s32[]{:S(2)}) async-start(), calls=%async_computation.4 | async-start | bytes 1638400 | tf_op jit(solution)/shard_map/all_gather | solution.py:40
  9.2 207.4 %all-gather.7.cloned.1.call-start = ((), (), s32[]{:S(2)}) async-start(), calls=%async_computation.5 | async-start | bytes 13107200 | tf_op jit(solution)/shard_map/all_gather | solution.py:32
  9.9 390.3 %all-gather.9.cloned.1.call-start = ((), (), s32[]{:S(2)}) async-start(), calls=%async_computation.6 | async-start | bytes 13107200 | tf_op jit(solution)/shard_map/all_gather | solution.py:33
  10.7 561.7 %all-reduce.7.cloned.1.call-start = ((), (), s32[]{:S(2)}) async-start(), calls=%async_computation.12 | async-start | bytes 13369344 | tf_op jit(solution)/shard_map/psum | solution.py:44
  412.2 211.3 %all-reduce.5.cloned.1.call-start = ((), (), s32[]{:S(2)}) async-start(), calls=%async_computation.11 | async-start | bytes 786432 | tf_op jit(solution)/shard_map/psum | solution.py:57
  572.4 4.7 copy-start.9
  577.0 5.4 copy-start.2
  577.0 2.0 copy-start.8
  577.0 3.2 copy-start.10
  582.4 1.3 copy-start.4
  585.1 8.8 copy-start.5
  585.1 58.4 %reduce-scatter.5.cloned.1.call-start = ((), (), s32[]{:S(2)}) async-start(), calls=%async_computation.7 | async-start | bytes 819200 | tf_op jit(solution)/shard_map/reduce_scatter | solution.py:54
  593.6 74.8 %reduce-scatter.7.cloned.1.call-start = ((), (), s32[]{:S(2)}) async-start(), calls=%async_computation.8 | async-start | bytes 819200 | tf_op jit(solution)/shard_map/reduce_scatter | solution.py:92
  601.7 247.8 %reduce-scatter.9.cloned.1.call-start = ((), (), s32[]{:S(2)}) async-start(), calls=%async_computation.9 | async-start | bytes 13107200 | tf_op jit(solution)/shard_map/reduce_scatter | solution.py:104
  608.5 423.0 %reduce-scatter.11.cloned.1.call-start = ((), (), s32[]{:S(2)}) async-start(), calls=%async_computation.10 | async-start | bytes 13107200 | tf_op jit(solution)/shard_map/reduce_scatter | solution.py:107
  617.0 3.8 copy-start.3
  620.8 412.0 %copy-start.1 = (bf16[1,256,4096]{2,1,0:T(8,128)(2,1)S(1)}, bf16[1,256,4096]{2,1,0:T(8,128)(2,1)}, u32[]{:S(2)}) copy-start(bf16[1,256,4096]{2,1,0:T(8,128)(2,1)} %param.15) | copy-start | bytes 6291460
  623.6 49.8 %copy-start.7 = (bf16[256,256]{1,0:T(8,128)(2,1)S(1)}, bf16[256,256]{1,0:T(8,128)(2,1)}, u32[]{:S(2)}) copy-start(bf16[256,256]{1,0:T(8,128)(2,1)} %get-tuple-element.9) | copy-start | bytes 393220
  644.8 31.1 %collective-permute-start = (bf16[1,64,1280]{2,1,0:T(8,128)(2,1)S(1)}, bf16[1,64,1280]{2,1,0:T(8,128)(2,1)S(1)}, u32[]{:S(2)}, u32[]{:S(2)}) collective-permute-start(bf16[1,64,1280]{2,1,0:T(8,128)(2,1)S(1)} %fusion.10), channel_id=1, source_target_pairs={{24,0},{0,8},{8,16},{16,24},{25,1},{1,9},{9,17},{17,25},{26,2},{2,... | collective-permute-start | bytes 491528 | tf_op jit(solution)/shard_map/ppermute | solution.py:10
  670.0 6.7 collective-permute-start.1
Sparse Core Ops, SparseCore 0:
  10.1 20.8 all-gather.4
  32.6 183.8 all-gather.6
  218.1 182.0 all-gather.8
  412.4 159.9 all-reduce.6
  585.2 32.8 all-reduce.4
  621.1 22.3 reduce-scatter.4
  646.0 22.3 reduce-scatter.6
  671.4 178.0 reduce-scatter.8
  852.4 179.0 reduce-scatter.10
where the time goes:
time: 1040 us
  waiting for transfers between devices  922 us (89%)
  matrix products  81.3 us (8%)
  between operations  14 us (1%)
    all_gather x1, waiting for transfers between devices, local(): lax.all_gather(shared_up, 'section', axis=1, tiled=True)  183 us
    reduce_scatter x1, waiting for transfers between devices, local(): lax.psum_scatter(grad_down.astype(jnp.bfloat16), 'section', scatter_dimen...  182 us
    all_gather x1, waiting for transfers between devices, local(): lax.all_gather(shared_down, 'section', axis=0, tiled=True)  174 us
    reduce_scatter x1, waiting for transfers between devices, local(): lax.psum_scatter(grad_up.astype(jnp.bfloat16), 'section', scatter_dimensi...  173 us
    psum x1, waiting for transfers between devices, local(): lax.psum(up_part.astype(jnp.bfloat16), 'row').astype(jnp.float32)  160 us
    reduce_scatter x1, waiting for transfers between devices, local(): lax.psum_scatter(gnorm_part.astype(jnp.bfloat16), 'col', scatter_dimensio...  22.1 us
  transfers between devices with their start and end apart: 11, of which 9 were waited for; matrix products, arithmetic and copies ran while one was open for 6% of the time, Pallas kernels for 0%

commit v1 on v0

v1 whole, which is shorter than its diff:
```python
import jax
import jax.numpy as jnp
from jax import lax
from jax.sharding import PartitionSpec as P

F32, BF16 = jnp.float32, jnp.bfloat16


def from_behind(block, axis, distance):
    count = lax.axis_size(axis)
    return lax.ppermute(block, axis, [((i - distance) % count, i) for i in range(count)])


def row_sum(part):
    total = part.astype(F32)
    for step in range(1, lax.axis_size("row")):
        total = total + from_behind(part, "row", step).astype(F32)
    return total


def row_gather(block, axis):
    count, me = lax.axis_size("row"), lax.axis_index("row")
    wide = jnp.zeros(block.shape[:axis] + (count * block.shape[axis],) + block.shape[axis + 1 :], block.dtype)
    for step in range(count):
        piece = block if step == 0 else from_behind(block, "row", step)
        origin = (me - step) % count
        wide = lax.dynamic_update_slice_in_dim(wide, piece, origin * block.shape[axis], axis)
    return wide


def mm(spec, left, right):
    return jnp.einsum(spec, left, right, preferred_element_type=F32)


def silu_slope(preact):
    sigma = jax.nn.sigmoid(preact)
    return sigma * (1.0 + preact * (1.0 - sigma))


def local(
    input_fwd,
    input_bwd,
    cotangent,
    shared_up,
    shared_down,
    up_left,
    up_right,
    down_left,
    down_right,
):
    sections, rows = lax.axis_size("section"), lax.axis_size("row")
    section, row = lax.axis_index("section"), lax.axis_index("row")
    own, width = input_fwd.shape[1], input_fwd.shape[2]
    units = shared_up.shape[1]
    share = up_left.shape[2] // rows
    everyone = ("section", "col")
    micro = own * lax.axis_size("col")

    def own_share(block, axis):
        return lax.dynamic_slice_in_dim(block, row * share, share, axis)

    def own_section(tokens):
        return lax.dynamic_slice_in_dim(tokens, section * micro, micro, 0)

    def per_section(tokens):
        return tokens.reshape(sections, micro, tokens.shape[-1])

    x_fwd, x_bwd, cot = input_fwd[0], input_bwd[0], cotangent[0]
    all_bwd = lax.all_gather(x_bwd, everyone, axis=0, tiled=True)
    all_cot = lax.all_gather(cot, everyone, axis=0, tiled=True)
    all_fwd = lax.all_gather(x_fwd, everyone, axis=0, tiled=True)

    din_part = mm("tmd,dr->tmr", jnp.stack([x_fwd, x_bwd]), up_left[0])
    gdout_part = mm("md,rd->mr", cot, down_right[0])
    low_part = jnp.concatenate([din_part, gdout_part[None]]).astype(BF16)
    low = own_share(row_sum(low_part).astype(BF16), 2)
    low_all = lax.all_gather(low, everyone, axis=1, tiled=True)
    din_fwd, din_bwd, gdout = (per_section(low_all[i]) for i in range(3))

    right = lax.all_to_all(own_share(up_right[0], 0), "section", 1, 0, tiled=True)
    right = right.reshape(sections, share, units)
    left = lax.all_to_all(own_share(down_left[0], 0 + 1), "section", 0, 0, tiled=True)
    left = left.reshape(sections, units, share)

    def preact_of(tokens, din):
        part = mm("smd,df->smf", per_section(tokens), shared_up) + mm("smr,srf->smf", din, right)
        return row_sum(part.astype(BF16))

    pre_bwd = preact_of(all_bwd, din_bwd)
    ghid_part = mm("smd,fd->smf", per_section(all_cot), shared_down) + mm("smr,sfr->smf", gdout, left)
    grad_hidden = row_sum(ghid_part.astype(BF16))
    hid_bwd = jax.nn.silu(pre_bwd).astype(BF16)
    gpre = (grad_hidden * silu_slope(pre_bwd)).astype(BF16)
    flat_gpre = gpre.reshape(sections * micro, units)

    gnorm_part = mm("mf,df->md", flat_gpre, shared_up)
    gdin_part = mm("smf,srf->smr", gpre, right).reshape(sections * micro, share)
    back_part = jnp.concatenate([gnorm_part.astype(BF16), gdin_part.astype(BF16)], axis=1)
    back = lax.psum_scatter(back_part, everyone, scatter_dimension=0, tiled=True)
    gdin_own = row_gather(back[:, width:], 1)

    pre_fwd = preact_of(all_fwd, din_fwd)
    hid_fwd = jax.nn.silu(pre_fwd).astype(BF16)
    out_part = mm("mf,fd->md", hid_fwd.reshape(sections * micro, units), shared_down)
    dout_part = [
        mm("smf,sfr->smr", h, left).reshape(sections * micro, share).astype(BF16) for h in (hid_fwd, hid_bwd)
    ]
    ahead_part = jnp.concatenate([out_part.astype(BF16), *dout_part], axis=1)
    ahead = lax.psum_scatter(ahead_part, everyone, scatter_dimension=0, tiled=True)
    dout_own = row_gather(ahead[:, width:].reshape(own, 2, share), 2)

    grad_up = mm("md,mf->df", all_bwd, flat_gpre).astype(BF16)
    grad_down = mm("mf,md->fd", hid_bwd.reshape(sections * micro, units), all_cot).astype(BF16)

    grad_left = mm("smf,smr->sfr", hid_bwd, gdout).astype(BF16).reshape(sections * units, share)
    grad_left = lax.all_to_all(grad_left, "section", 0, 0, tiled=True)
    grad_down_left = row_gather(grad_left, 1).astype(F32)
    grad_right = mm("smr,smf->srf", din_bwd, gpre).astype(BF16).reshape(sections * share, units)
    grad_right = lax.all_to_all(grad_right, "section", 0, 1, tiled=True)
    grad_up_right = row_gather(grad_right, 0).astype(F32)

    grad_input = (
        cot.astype(F32) + back[:, :width].astype(F32) + mm("mr,dr->md", gdin_own, up_left[0])
    )
    handoff_bwd = from_behind(grad_input.astype(BF16)[None], "section", -1)
    gdin_all = lax.all_gather(gdin_own, "col", axis=0, tiled=True)
    grad_up_left = mm("md,mr->dr", own_section(all_bwd), gdin_all)

    out_fwd = (
        x_fwd.astype(F32) + ahead[:, :width].astype(F32) + mm("mr,rd->md", dout_own[:, 0], down_right[0])
    )
    handoff_fwd = from_behind(out_fwd.astype(BF16)[None], "section", 1)
    dout_all = lax.all_gather(dout_own[:, 1], "col", axis=0, tiled=True)
    grad_down_right = mm("mr,md->rd", dout_all, own_section(all_cot))
    return (
        handoff_fwd,
        handoff_bwd,
        grad_up,
        grad_down,
        grad_up_left[None],
        grad_up_right[None],
        grad_down_left[None],
        grad_down_right[None],
    )


def solution(mesh):
    in_specs = (
        P("section", "col", "row"),
        P("section", "col", "row"),
        P("section", "col", "row"),
        P("row", ("col", "section")),
        P(("col", "section"), "row"),
        P("section", "row", None),
        P("section", None, "col"),
        P("section", "col", None),
        P("section", None, "row"),
    )
    out_specs = (
        P("section", "col", "row"),
        P("section", "col", "row"),
        P("row", ("col", "section")),
        P(("col", "section"), "row"),
        P("section", "row", None),
        P("section", None, "col"),
        P("section", "col", None),
        P("section", None, "row"),
    )
    return jax.shard_map(local, mesh=mesh, in_specs=in_specs, out_specs=out_specs, check_vma=False)
```

time: 1040 us -> 363 us (0.35)
  waiting for transfers between devices: 922 us -> 143 us
  blocking collectives: 9.6 us -> 43.5 us
  starting transfers between devices: 5.47 us -> 37.7 us
  local copies, waits for them, and re-layouts: 5.57 us -> 34.7 us
  other arithmetic: 1.93 us -> 19.6 us
  matrix products: 81.3 us -> 68.4 us
    reduce_scatter x4 -> x2, waiting for transfers between devices: 393 us -> 0.01 us  [the longest x1 0.01 us: local(): lax.psum_scatter(back_part, everyone, scatter_dimension=0, tiled=True)]
    all_gather x3, waiting for transfers between devices: 366 us -> 71.9 us  [the longest x1 40 us: local(): all_bwd = lax.all_gather(x_bwd, everyone, axis=0, tiled=True)]
    psum x2 -> x0, waiting for transfers between devices: 160 us -> none  [the longest x1 160 us: local(): lax.psum(up_part.astype(jnp.bfloat16), 'row').astype(jnp.float32)]
    ppermute x2 -> x10, waiting for transfers between devices: 0.75 us -> 59.7 us  [from_behind(): lax.ppermute(block, axis, [((i - distance) % count, i) for i in range(cou...]
    all_gather x1 -> x3, blocking collectives: 9.6 us -> 43.5 us  [the longest x1 32.7 us: local(): low_all = lax.all_gather(low, everyone, axis=1, tiled=True)]
    all_to_all x0 -> x4, starting transfers between devices: none -> 23.1 us  [the longest x1 8.06 us: local(): lax.all_to_all(own_share(up_right[0], 0), 'section', 1, 0, tiled=True)]
    dot_general x18 -> x21, matrix products: 81.3 us -> 68.4 us  [mm(): return jnp.einsum(spec, left, right, preferred_element_type=F32)]
  transfers between devices with their start and end apart: 11 -> 19, of which waited for: 9 -> 7; matrix products, arithmetic and copies ran while one was open for 6% -> 28% of each run, Pallas kernels for 0% -> 0%
where the time goes in v1:
time: 363 us; the launch traced here: 362 us
  waiting for transfers between devices  143 us (39%)
  matrix products  68.4 us (19%)
  blocking collectives  43.5 us (12%)
  starting transfers between devices  37.7 us (10%)
  local copies, waits for them, and re-layouts  34.7 us (10%)
  other arithmetic  19.6 us (5%)
  between operations  14.1 us (4%)
    dot_general x21, matrix products, mm(): return jnp.einsum(spec, left, right, preferred_element_type=F32)  68.4 us
    ppermute x10, waiting for transfers between devices, from_behind(): lax.ppermute(block, axis, [((i - distance) % count, i) for i in range(cou...  59.7 us
    all_gather x1, waiting for transfers between devices, local(): all_bwd = lax.all_gather(x_bwd, everyone, axis=0, tiled=True)  40 us
    all_gather x1, blocking collectives, local(): low_all = lax.all_gather(low, everyone, axis=1, tiled=True)  32.7 us
    all_gather x1, waiting for transfers between devices, local(): all_fwd = lax.all_gather(x_fwd, everyone, axis=0, tiled=True)  31.9 us
    ppermute x10, starting transfers between devices, from_behind(): lax.ppermute(block, axis, [((i - distance) % count, i) for i in range(cou...  14.5 us
    unnamed x42, local copies, waits for them, and re-layouts  12.3 us
    all_to_all x1, waiting for transfers between devices, local(): grad_left = lax.all_to_all(grad_left, 'section', 0, 0, tiled=True)  9.72 us
  transfers between devices with their start and end apart: 19, of which 7 were waited for; matrix products, arithmetic and copies ran while one was open for 28% of the time, Pallas kernels for 0%

profile of v1, /device:TPU:0, one launch (start us, length us, event | category | flops | bytes accessed | tf_op | source)
XLA Modules:
  0.0 361.5 jit_solution(5523919161392895789)
XLA Ops:
  11.0 6.3 %all-to-all-start.1 = ((bf16[4,1024,128]{2,1,0:T(8,128)(2,1)}), bf16[4,1024,128]{2,1,0:T(8,128)(2,1)}, u32[]{:S(2)}, u32[]{:S(2)}) async-start(bf16[4,1024,128]{2,1,0:T(8,128)(2,1)} %bitcast.122), calls=%async_computation.1 | async-start | bytes 2097152 | tf_op jit(solution)/shard_map/all_to_all | solution.py:82
  28.1 32.7 %all_gather.19 = bf16[3,1024,128]{2,1,0:T(8,128)(2,1)S(1)} all-gather(bf16[3,64,128]{2,1,0:T(8,128)(2,1)S(1)} %add_convert_fusion.3), channel_id=1, replica_groups=mesh['section'=4,'row'=2,'col'=4] {'section','col'}, dimensions={1}, use_global_device_ids=true | all-gather | bytes 835584 | tf_op jit(solution)/shard_map/all_gather | solution.py:77
  61.6 8.1 %all-to-all-start = ((bf16[128,4,1024]{2,0,1:T(8,128)(2,1)}), bf16[128,4,1024]{2,0,1:T(8,128)(2,1)}, u32[]{:S(2)}, u32[]{:S(2)}) async-start(bf16[128,4,1024]{2,0,1:T(8,128)(2,1)} %copy.21), calls=%async_computation | async-start | bytes 2097152 | tf_op jit(solution)/shard_map/all_to_all | solution.py:80
  69.7 5.4 %fusion.3 = f32[4,256,1024]{2,1,0:T(8,128)S(1)} fusion(bf16[4,256,1280]{2,1,0:T(8,128)(2,1)} %bitcast.135, bf16[1024,1280]{1,0:T(8,128)(2,1)} %param.13), kind=kOutput, calls=%fused_computation.19 | convolution fusion | flops 2684354560 | bytes 9437184 | tf_op jit(solution)/shard_map/smd,fd->smf/dot_general | solution.py:32
  75.1 3.3 add_convert_fusion
  79.9 40.0 %all-gather.10.cloned.1.call-done = bf16[1,1024,1280]{2,1,0:T(8,128)(2,1)} async-done(((bf16[1,64,1280]{2,1,0:T(8,128)(2,1)}), bf16[1,1024,1280]{2,1,0:T(8,128)(2,1)}) %all-gather.10.cloned.1.call-update) | async-done | bytes 2621456 | tf_op jit(solution)/shard_map/all_gather | solution.py:69
  119.8 6.1 %fusion.5 = f32[4,256,1024]{2,1,0:T(8,128)} fusion(bf16[4,256,1280]{2,1,0:T(8,128)(2,1)} %bitcast.136, bf16[1280,1024]{1,0:T(8,128)(2,1)S(1)} %copy-done), kind=kOutput, calls=%fused_computation.21 | convolution fusion | flops 2684354560 | bytes 9437184 | tf_op jit(solution)/shard_map/smd,df->smf/dot_general | solution.py:32
  126.0 4.7 %add_convert_fusion.1 = bf16[4,256,1024]{2,1,0:T(8,128)(2,1)} fusion(f32[4,256,1024]{2,1,0:T(8,128)} %fusion.5, bf16[4,256,128]{2,1,0:T(8,128)(2,1)} %bitcast.128, bf16[128,4,1024]{2,0,1:T(8,128)(2,1)} %all-to-all-done), kind=kOutput, calls=%fused_computation.5 | convolution fusion | flops 270532608 | bytes 7602176 | tf_op jit(solution)/shard_map/smr,srf->smf/dot_general | solution.py:32
  132.1 31.9 %all-gather.8.cloned.1.call-done = bf16[1,1024,1280]{2,1,0:T(8,128)(2,1)} async-done(((bf16[1,64,1280]{2,1,0:T(8,128)(2,1)}), bf16[1,1024,1280]{2,1,0:T(8,128)(2,1)}) %all-gather.8.cloned.1.call-update) | async-done | bytes 2621456 | tf_op jit(solution)/shard_map/all_gather | solution.py:71
  164.0 6.1 %fusion.7 = f32[4,256,1024]{2,1,0:T(8,128)} fusion(bf16[4,256,1280]{2,1,0:T(8,128)(2,1)} %bitcast.137, bf16[1280,1024]{1,0:T(8,128)(2,1)S(1)} %copy-done), kind=kOutput, calls=%fused_computation.23 | convolution fusion | flops 2684354560 | bytes 9437184 | tf_op jit(solution)/shard_map/smd,df->smf/dot_general | solution.py:32
  170.1 8.6 %collective-permute-done.2 = bf16[4,256,1024]{2,1,0:T(8,128)(2,1)} collective-permute-done((bf16[4,256,1024]{2,1,0:T(8,128)(2,1)}, bf16[4,256,1024]{2,1,0:T(8,128)(2,1)}, u32[]{:S(2)}, u32[]{:S(2)}) %collective-permute-start.2) | collective-permute-done | bytes 2097184 | tf_op jit(solution)/shard_map/ppermute | solution.py:11
  178.7 5.7 %multiply_convert_fusion = (bf16[4,256,1024]{2,1,0:T(8,128)(2,1)S(1)}, bf16[4,256,1024]{2,1,0:T(8,128)(2,1)}) fusion(bf16[4,256,1024]{2,1,0:T(8,128)(2,1)} %collective-permute-done.5, bf16[4,256,1024]{2,1,0:T(8,128)(2,1)} %add_convert_fusion, bf16[4,256,1024]{2,1,0:T(8,128)(2,1)} %collective-permute-done.2, bf16[4,256,1024]{2,1,0:T(8,128)(2,1)} %add_convert_fusion.1), kind=kLoop, calls=%fused_computation | loop fusion | flops 17825792 | bytes 12582912 | tf_op jit(solution)/shard_map/convert_element_type | solution.py:93
  184.3 3.1 convolution_convert_fusion.2
  192.2 3.3 add_convert_fusion.2
  198.5 4.5 %all-to-all-start.2 = ((bf16[4,128,1024]{2,1,0:T(8,128)(2,1)}), bf16[4,128,1024]{2,1,0:T(8,128)(2,1)}, u32[]{:S(2)}, u32[]{:S(2)}) async-start(bf16[4,128,1024]{2,1,0:T(8,128)(2,1)} %convolution_convert_fusion.5), calls=%async_computation.4 | async-start | bytes 2097152 | tf_op jit(solution)/shard_map/all_to_all | solution.py:119
  203.0 3.7 %convolution_convert_fusion.4 = bf16[4,1024,128]{2,1,0:T(8,128)(2,1)} fusion(bf16[4,256,1024]{2,1,0:T(8,128)(2,1)} %get-tuple-element.25, bf16[4,256,128]{2,1,0:T(8,128)(2,1)S(1)} %bitcast.127), kind=kOutput, calls=%fused_computation.31 | convolution fusion | flops 268959744 | bytes 3407872 | tf_op jit(solution)/shard_map/smf,smr->sfr/dot_general | solution.py:32
  208.7 33.9 %collective-permute-done.1 = bf16[4,256,1024]{2,1,0:T(8,128)(2,1)} collective-permute-done((bf16[4,256,1024]{2,1,0:T(8,128)(2,1)S(1)}, bf16[4,256,1024]{2,1,0:T(8,128)(2,1)}, u32[]{:S(2)}, u32[]{:S(2)}) %collective-permute-start.1) | collective-permute-done | bytes 2097184 | tf_op jit(solution)/shard_map/ppermute | solution.py:11
  242.6 2.9 multiply_convert_fusion.2
  246.9 3.1 convolution_convert_fusion.3
  249.9 4.2 %all-to-all-start.3 = ((bf16[4,1024,128]{2,1,0:T(8,128)(2,1)}), bf16[4,1024,128]{2,1,0:T(8,128)(2,1)}, u32[]{:S(2)}, u32[]{:S(2)}) async-start(bf16[4,1024,128]{2,1,0:T(8,128)(2,1)} %convolution_convert_fusion.4), calls=%async_computation.5 | async-start | bytes 2097152 | tf_op jit(solution)/shard_map/all_to_all | solution.py:116
  254.2 2.6 convolution_convert_fusion.8
  258.8 6.9 %fusion = bf16[1280,1024]{0,1:T(8,128)(2,1)} fusion(bf16[1024,1024]{1,0:T(8,128)(2,1)} %bitcast.121, bf16[1,1024,1280]{2,1,0:T(8,128)(2,1)} %all-gather.10.cloned.1.call-done), kind=kOutput, calls=%fused_computation.12 | convolution fusion | flops 2685665280 | bytes 7340032 | tf_op jit(solution)/shard_map/md,mf->df/dot_general | solution.py:32
  269.3 9.7 %all-to-all-done.3 = bf16[4,1024,128]{2,1,0:T(8,128)(2,1)} async-done(((bf16[4,1024,128]{2,1,0:T(8,128)(2,1)}), bf16[4,1024,128]{2,1,0:T(8,128)(2,1)}, u32[]{:S(2)}, u32[]{:S(2)}) %all-to-all-start.3) | async-done | bytes 1048608 | tf_op jit(solution)/shard_map/all_to_all | solution.py:116
  280.5 6.0 %convolution_convert_fusion = bf16[1024,1280]{1,0:T(8,128)(2,1)} fusion(bf16[1024,1024]{1,0:T(8,128)(2,1)S(1)} %bitcast.119, bf16[1,1024,1280]{2,1,0:T(8,128)(2,1)} %all-gather.12.cloned.1.call-done), kind=kOutput, calls=%fused_computation.8 | convolution fusion | flops 2685665280 | bytes 7340032 | tf_op jit(solution)/shard_map/mf,md->fd/dot_general | solution.py:32
  286.5 4.5 %copy.30 = bf16[1280,1024]{1,0:T(8,128)(2,1)} copy(bf16[1280,1024]{0,1:T(8,128)(2,1)} %fusion) | data formatting | bytes 5242880
  299.8 14.5 %collective-permute-done.9 = bf16[4096,128]{1,0:T(8,128)(2,1)} collective-permute-done((bf16[4096,128]{1,0:T(8,128)(2,1)}, bf16[4096,128]{1,0:T(8,128)(2,1)}, u32[]{:S(2)}, u32[]{:S(2)}) %collective-permute-start.9) | collective-permute-done | bytes 1048608 | tf_op jit(solution)/shard_map/ppermute | solution.py:11
  322.8 4.0 %broadcast_in_dim.57 = f32[1,4096,256]{2,1,0:T(8,128)} convert(bf16[1,4096,256]{2,1,0:T(8,128)(2,1)} %bitcast_dynamic-update-slice_fusion) | non-fusion elementwise | flops 1048576 | bytes 6291456 | tf_op jit(solution)/shard_map/broadcast_in_dim | solution.py:142
  327.2 3.5 collective-permute-start.7
  330.7 5.4 %all_gather.22 = bf16[256,256]{1,0:T(8,128)(2,1)S(1)} all-gather(bf16[64,256]{1,0:T(8,128)(2,1)S(1)} %constant_dynamic-update-slice_fusion.2), channel_id=1, replica_groups=mesh['section'=4,'row'=2,'col'=4] {'col'}, dimensions={0}, use_global_device_ids=true | all-gather | bytes 163840 | tf_op jit(solution)/shard_map/all_gather | solution.py:126
  336.1 2.7 convolution_bitcast_fusion.1
  340.8 2.7 collective-permute-done.3
  344.8 5.4 %all-gather.3 = bf16[256,1,256]{2,0,1:T(8,128)(2,1)S(1)} all-gather(bf16[64,1,256]{2,0,1:T(8,128)(2,1)S(1)} %slice.44), channel_id=5, replica_groups=mesh['section'=4,'row'=2,'col'=4] {'col'}, dimensions={0}, use_global_device_ids=true | all-gather | bytes 163840 | tf_op jit(solution)/shard_map/all_gather | solution.py:133
  (106 shorter events, 62.0 us)
Async XLA Ops:
  7.2 112.7 %copy-start = (bf16[1280,1024]{1,0:T(8,128)(2,1)S(1)}, bf16[1280,1024]{1,0:T(8,128)(2,1)}, u32[]{:S(2)}) copy-start(bf16[1280,1024]{1,0:T(8,128)(2,1)} %param.12) | copy-start | bytes 7864324
  7.2 10.9 %copy-start.11 = (bf16[1,64,1280]{2,1,0:T(8,128)(2,1)S(1)}, bf16[1,64,1280]{2,1,0:T(8,128)(2,1)}, u32[]{:S(2)}) copy-start(bf16[1,64,1280]{2,1,0:T(8,128)(2,1)} %param.11) | copy-start | bytes 491524
  7.2 10.8 %copy-start.8 = (bf16[1,256,1280]{2,1,0:T(8,128)(2,1)S(1)}, bf16[1,256,1280]{2,1,0:T(8,128)(2,1)}, u32[]{:S(2)}) copy-start(bf16[1,256,1280]{2,1,0:T(8,128)(2,1)} %param.17) | copy-start | bytes 1966084
  7.2 62.5 %all-gather.12.cloned.1.call-start = ((), (), s32[]{:S(2)}) async-start(), calls=%async_computation.10 | async-start | bytes 2785280 | tf_op jit(solution)/shard_map/all_gather | solution.py:70
  7.9 111.9 %all-gather.10.cloned.1.call-start = ((), (), s32[]{:S(2)}) async-start(), calls=%async_computation.9 | async-start | bytes 2785280 | tf_op jit(solution)/shard_map/all_gather | solution.py:69
  11.0 50.6 %all-to-all-start.1 = ((bf16[4,1024,128]{2,1,0:T(8,128)(2,1)}), bf16[4,1024,128]{2,1,0:T(8,128)(2,1)}, u32[]{:S(2)}, u32[]{:S(2)}) async-start(bf16[4,1024,128]{2,1,0:T(8,128)(2,1)} %bitcast.122), calls=%async_computation.1 | async-start | bytes 2097152 | tf_op jit(solution)/shard_map/all_to_all | solution.py:82
  17.3 146.6 %all-gather.8.cloned.1.call-start = ((), (), s32[]{:S(2)}) async-start(), calls=%async_computation.8 | async-start | bytes 2785280 | tf_op jit(solution)/shard_map/all_gather | solution.py:71
  20.1 7.1 %collective-permute-start = (bf16[3,64,256]{2,1,0:T(8,128)(2,1)S(1)}, bf16[3,64,256]{2,1,0:T(8,128)(2,1)}, u32[]{:S(2)}, u32[]{:S(2)}) collective-permute-start(bf16[3,64,256]{2,1,0:T(8,128)(2,1)S(1)} %pad_maximum_fusion.2), channel_id=1, source_target_pairs={{4,0},{0,4},{5,1},{1,5},{6,2},{2,6},{7,3},{3,7},{12,8},{8,12},{13,... | collective-permute-start | bytes 294920 | tf_op jit(solution)/shard_map/ppermute | solution.py:11
  61.6 64.4 %all-to-all-start = ((bf16[128,4,1024]{2,0,1:T(8,128)(2,1)}), bf16[128,4,1024]{2,0,1:T(8,128)(2,1)}, u32[]{:S(2)}, u32[]{:S(2)}) async-start(bf16[128,4,1024]{2,0,1:T(8,128)(2,1)} %copy.21), calls=%async_computation | async-start | bytes 2097152 | tf_op jit(solution)/shard_map/all_to_all | solution.py:80
  69.7 246.9 %reduce-scatter.5.cloned.1.call-start = ((), (), s32[]{:S(2)}) async-start(), calls=%async_computation.7 | async-start | bytes 3063808 | tf_op jit(solution)/shard_map/reduce_scatter | solution.py:99
  78.4 91.7 %collective-permute-start.5 = (bf16[4,256,1024]{2,1,0:T(8,128)(2,1)}, bf16[4,256,1024]{2,1,0:T(8,128)(2,1)}, u32[]{:S(2)}, u32[]{:S(2)}) collective-permute-start(bf16[4,256,1024]{2,1,0:T(8,128)(2,1)} %add_convert_fusion), channel_id=1, source_target_pairs={{4,0},{0,4},{5,1},{1,5},{6,2},{2,6},{7,3},{3,7},{12,8},{8,12},{13,... | collective-permute-start | bytes 6291464 | tf_op jit(solution)/shard_map/ppermute | solution.py:11
  130.6 48.1 %collective-permute-start.2 = (bf16[4,256,1024]{2,1,0:T(8,128)(2,1)}, bf16[4,256,1024]{2,1,0:T(8,128)(2,1)}, u32[]{:S(2)}, u32[]{:S(2)}) collective-permute-start(bf16[4,256,1024]{2,1,0:T(8,128)(2,1)} %add_convert_fusion.1), channel_id=1, source_target_pairs={{4,0},{0,4},{5,1},{1,5},{6,2},{2,6},{7,3},{3,7},{12,8},{8,12},{13,... | collective-permute-start | bytes 6291464 | tf_op jit(solution)/shard_map/ppermute | solution.py:11
  192.2 4.9 %copy-start.5 = (bf16[4,256,1024]{2,1,0:T(8,128)(2,1)S(1)}, bf16[4,256,1024]{2,1,0:T(8,128)(2,1)}, u32[]{:S(2)}) copy-start(bf16[4,256,1024]{2,1,0:T(8,128)(2,1)} %copy-done.4) | copy-start | bytes 6291460
  192.2 4.9 %copy-start.9 = (bf16[1,1024,128]{2,1,0:T(8,128)(2,1)S(1)}, bf16[1,1024,128]{2,1,0:T(8,128)(2,1)}, u32[]{:S(2)}) copy-start(bf16[1,1024,128]{2,1,0:T(8,128)(2,1)} %get-tuple-element.27) | copy-start | bytes 786436
  195.5 47.1 %collective-permute-start.1 = (bf16[4,256,1024]{2,1,0:T(8,128)(2,1)S(1)}, bf16[4,256,1024]{2,1,0:T(8,128)(2,1)}, u32[]{:S(2)}, u32[]{:S(2)}) collective-permute-start(bf16[4,256,1024]{2,1,0:T(8,128)(2,1)S(1)} %add_convert_fusion.2), channel_id=1, source_target_pairs={{4,0},{0,4},{5,1},{1,5},{6,2},{2,6},{7,3},{3,7},{12,8},{8,12},{13,... | collective-permute-start | bytes 6291464 | tf_op jit(solution)/shard_map/ppermute | solution.py:11
  198.5 51.4 %all-to-all-start.2 = ((bf16[4,128,1024]{2,1,0:T(8,128)(2,1)}), bf16[4,128,1024]{2,1,0:T(8,128)(2,1)}, u32[]{:S(2)}, u32[]{:S(2)}) async-start(bf16[4,128,1024]{2,1,0:T(8,128)(2,1)} %convolution_convert_fusion.5), calls=%async_computation.4 | async-start | bytes 2097152 | tf_op jit(solution)/shard_map/all_to_all | solution.py:119
  208.7 38.1 %copy-start.18 = (bf16[1024,1280]{1,0:T(8,128)(2,1)S(1)}, bf16[1024,1280]{1,0:T(8,128)(2,1)}, u32[]{:S(2)}) copy-start(bf16[1024,1280]{1,0:T(8,128)(2,1)} %param.13) | copy-start | bytes 7864324
  249.9 29.1 %all-to-all-start.3 = ((bf16[4,1024,128]{2,1,0:T(8,128)(2,1)}), bf16[4,1024,128]{2,1,0:T(8,128)(2,1)}, u32[]{:S(2)}, u32[]{:S(2)}) async-start(bf16[4,1024,128]{2,1,0:T(8,128)(2,1)} %convolution_convert_fusion.4), calls=%async_computation.5 | async-start | bytes 2097152 | tf_op jit(solution)/shard_map/all_to_all | solution.py:116
  254.2 84.6 %reduce-scatter.3.cloned.1.call-start = ((), (), s32[]{:S(2)}) async-start(), calls=%async_computation.6 | async-start | bytes 3342336 | tf_op jit(solution)/shard_map/reduce_scatter | solution.py:109
  258.8 21.8 %copy-start.3 = (bf16[4,256,1024]{2,1,0:T(8,128)(2,1)S(1)}, bf16[4,256,1024]{2,1,0:T(8,128)(2,1)}, u32[]{:S(2)}) copy-start(bf16[4,256,1024]{2,1,0:T(8,128)(2,1)} %get-tuple-element.25) | copy-start | bytes 6291460
  268.0 29.5 %collective-permute-start.8 = (bf16[128,4096]{0,1:T(8,128)(2,1)}, bf16[128,4096]{0,1:T(8,128)(2,1)}, u32[]{:S(2)}, u32[]{:S(2)}) collective-permute-start(bf16[128,4096]{0,1:T(8,128)(2,1)} %bitcast.123), channel_id=1, source_target_pairs={{4,0},{0,4},{5,1},{1,5},{6,2},{2,6},{7,3},{3,7},{12,8},{8,12},{13,... | collective-permute-start | bytes 3145736 | tf_op jit(solution)/shard_map/ppermute | solution.py:11
  279.1 35.2 %collective-permute-start.9 = (bf16[4096,128]{1,0:T(8,128)(2,1)}, bf16[4096,128]{1,0:T(8,128)(2,1)}, u32[]{:S(2)}, u32[]{:S(2)}) collective-permute-start(bf16[4096,128]{1,0:T(8,128)(2,1)} %bitcast.36), channel_id=1, source_target_pairs={{4,0},{0,4},{5,1},{1,5},{6,2},{2,6},{7,3},{3,7},{12,8},{8,12},{13,... | collective-permute-start | bytes 3145736 | tf_op jit(solution)/shard_map/ppermute | solution.py:11
  286.5 4.5 %copy-start.7 = (bf16[128,4,1024]{0,2,1:T(8,128)(2,1)S(1)}, bf16[128,4,1024]{0,2,1:T(8,128)(2,1)}, u32[]{:S(2)}) copy-start(bf16[128,4,1024]{0,2,1:T(8,128)(2,1)} %copy.25) | copy-start | bytes 3145732
  317.3 9.5 %collective-permute-start.6 = (bf16[64,128]{1,0:T(8,128)(2,1)S(1)}, bf16[64,128]{1,0:T(8,128)(2,1)S(1)}, u32[]{:S(2)}, u32[]{:S(2)}) collective-permute-start(bf16[64,128]{1,0:T(8,128)(2,1)S(1)} %get-tuple-element.29), channel_id=1, source_target_pairs={{4,0},{0,4},{5,1},{1,5},{6,2},{2,6},{7,3},{3,7},{12,8},{8,12},{13,... | collective-permute-start | bytes 49160 | tf_op jit(solution)/shard_map/ppermute | solution.py:11
  322.8 4.0 %copy-start.12 = (bf16[1,64,1280]{2,1,0:T(8,128)(2,1)S(1)}, bf16[1,64,1280]{2,1,0:T(8,128)(2,1)}, u32[]{:S(2)}) copy-start(bf16[1,64,1280]{2,1,0:T(8,128)(2,1)} %param.11) | copy-start | bytes 491524
  322.8 4.0 %copy-start.15 = (bf16[1,1280,256]{2,1,0:T(8,128)(2,1)S(1)}, bf16[1,1280,256]{2,1,0:T(8,128)(2,1)}, u32[]{:S(2)}) copy-start(bf16[1,1280,256]{2,1,0:T(8,128)(2,1)} %param.14) | copy-start | bytes 1966084
  322.8 4.1 %copy-start.17 = (bf16[64,1408]{1,0:T(8,128)(2,1)S(1)}, bf16[64,1408]{1,0:T(8,128)(2,1)}, u32[]{:S(2)}) copy-start(bf16[64,1408]{1,0:T(8,128)(2,1)} %reduce-scatter.5.cloned.1.call-done) | copy-start | bytes 540676
  326.8 16.7 %copy-start.14 = (bf16[1,64,1280]{2,1,0:T(8,128)(2,1)S(1)}, bf16[1,64,1280]{2,1,0:T(8,128)(2,1)}, u32[]{:S(2)}) copy-start(bf16[1,64,1280]{2,1,0:T(8,128)(2,1)} %param.9) | copy-start | bytes 491524
  327.2 11.6 %collective-permute-start.7 = (bf16[1,64,1280]{2,1,0:T(8,128)(2,1)S(1)}, bf16[1,64,1280]{2,1,0:T(8,128)(2,1)}, u32[]{:S(2)}, u32[]{:S(2)}) collective-permute-start(bf16[1,64,1280]{2,1,0:T(8,128)(2,1)S(1)} %fusion.11), channel_id=1, source_target_pairs={{8,0},{16,8},{24,16},{0,24},{9,1},{17,9},{25,17},{1,25},{10,2},{18... | collective-permute-start | bytes 491528 | tf_op jit(solution)/shard_map/ppermute | solution.py:11
  336.1 18.9 %copy-start.1 = (bf16[1280,1024]{1,0:T(8,128)(2,1)S(1)}, bf16[1280,1024]{1,0:T(8,128)(2,1)}, u32[]{:S(2)}) copy-start(bf16[1280,1024]{1,0:T(8,128)(2,1)} %param.12) | copy-start | bytes 7864324
  339.6 3.9 %collective-permute-start.3 = (bf16[64,2,128]{2,0,1:T(8,128)(2,1)S(1)}, bf16[64,2,128]{2,0,1:T(8,128)(2,1)S(1)}, u32[]{:S(2)}, u32[]{:S(2)}) collective-permute-start(bf16[64,2,128]{2,0,1:T(8,128)(2,1)S(1)} %copy_bitcast_fusion), channel_id=1, source_target_pairs={{4,0},{0,4},{5,1},{1,5},{6,2},{2,6},{7,3},{3,7},{12,8},{8,12},{13,... | collective-permute-start | bytes 98312 | tf_op jit(solution)/shard_map/ppermute | solution.py:11
  344.7 8.0 %collective-permute-start.4 = (bf16[1,64,1280]{2,1,0:T(8,128)(2,1)S(1)}, bf16[1,64,1280]{2,1,0:T(8,128)(2,1)S(1)}, u32[]{:S(2)}, u32[]{:S(2)}) collective-permute-start(bf16[1,64,1280]{2,1,0:T(8,128)(2,1)S(1)} %fusion.12), channel_id=1, source_target_pairs={{24,0},{0,8},{8,16},{16,24},{25,1},{1,9},{9,17},{17,25},{26,2},{2,... | collective-permute-start | bytes 491528 | tf_op jit(solution)/shard_map/ppermute | solution.py:11
  (6 other events, 14.0 us)
Sparse Core Ops, SparseCore 0:
  10.3 59.3 all-gather.11
  72.0 47.8 all-gather.9
  122.1 41.7 all-gather.7
  191.4 65.7 reduce-scatter.4
  260.9 65.5 reduce-scatter.2
